TPU v7x, 256 devices: a whole 4x4x8 slice. The times are simulated.
256 devices in a mesh: col: 8 (over z_lo, core), dp: 32 (over z_hi, y, x).
Axes of the slice: x: 4, y: 4, z: 8 (z_hi: 2, z_lo: 4; z = z_hi * 4 + z_lo), core: 2. Of those that a mesh axis runs over, the one named last changes fastest.
Arguments:
- acts: bfloat16 [12288, 5120], P('dp', 'col'), may hold values from -6 to 6
- out_grad: bfloat16 [12288, 8192], P('dp', 'col'), may hold values from -6 to 6
- projection: bfloat16 [5120, 256], replicated, may hold values from -0.078125 to 0.078125
- weight: bfloat16 [5120, 8192], P('dp', 'col'), may hold values from -0.078125 to 0.078125
- m_codes: int32 [256, 8192], P('dp', 'col'), may hold values from -127 to 127
- m_exps: int32 [256, 256], P('dp', 'col'), may hold values from -16 to -9
- v_codes: int32 [256, 8192], P('dp', 'col'), may hold values from 1 to 127
- v_exps: int32 [256, 256], P('dp', 'col'), may hold values from -24 to -18
- next_acts: bfloat16 [12288, 5120], P('dp', 'col'), may hold values from -6 to 6
Outputs:
- next_out: bfloat16 [12288, 8192], P('dp', 'col')
- new_weight: bfloat16 [5120, 8192], P('dp', 'col')
- update: float32 [256, 8192], P('dp', 'col')
Inputs may be any that keep to these rules, and one draw needn't show every extreme that they name: `v_codes`: second moment mantissas are positive.
All inputs are finite; a program needn't handle non-finite values.
Results may differ from a plain program's by a relative error of at most 0.0051.
Values may be sent and summed in bfloat16 or wider, within the bound.
No kernel may reach another device: no remote copies, remote signals or barrier semaphores. Data moves between devices by JAX's collectives and lax.ppermute only.
A program may use at most 128 MiB of HBM per device.

v0:
```python
import jax
import jax.numpy as jnp
from jax import lax
from jax.sharding import Mesh
from jax.sharding import PartitionSpec as P

DP = ("dp_0", "dp_1", "dp_2")
learn_rate = 0.02
beta_one = 0.9
beta_two = 0.999
epsilon = 1e-08
correct_first = 0.9999734386011124
correct_second = 0.0952078528862904


def sent_to_all(shard, axis):
    size = lax.axis_size(axis)
    return lax.all_to_all(
        jnp.broadcast_to(shard[None], (size, *shard.shape)), axis, 0, 0, tiled=True
    )


def over_copies(shard, axis):
    everything = sent_to_all(shard, axis)
    return jnp.sum(everything, axis=0)


def cut_along(shard, dim, size):
    shape = shard.shape
    pieces = shard.reshape(*shape[:dim], size, shape[dim] // size, *shape[dim + 1 :])
    return jnp.moveaxis(pieces, dim, 0)


def sum_at_owner(shard, axis, dim):
    pieces = cut_along(shard, dim, lax.axis_size(axis))
    arrived = lax.all_to_all(pieces, axis, split_axis=0, concat_axis=0, tiled=True)
    return arrived.sum(axis=0)


def joined_along(pieces, dim):
    shape = list(pieces.shape[1:])
    shape[dim] *= pieces.shape[0]
    return jnp.moveaxis(pieces, 0, dim).reshape(shape)


def gather_in_order(shard, axes, sequence):
    pieces = shard[None]
    for k in sequence:
        pieces = lax.all_gather(pieces, axes[k], axis=0, tiled=True)
    block = [lax.axis_size(axes[k]) for k in reversed(sequence)]
    pieces = pieces.reshape(*block, *shard.shape)
    turned = sorted(range(len(sequence)), key=lambda place: sequence[len(sequence) - 1 - place])
    return pieces.transpose(*turned, *range(len(sequence), pieces.ndim)).reshape(-1, *shard.shape)


def gathered_by_axis(shard, axes, sequence, dim):
    return joined_along(gather_in_order(shard, axes, sequence), dim)


def collect(shard, axis, dim):
    pieces = sent_to_all(shard, axis)
    return joined_along(pieces, dim)


def decode(codes, exps):
    scale = jnp.exp2(exps.astype(jnp.float32))
    rows = codes.shape[0]
    values = (codes.astype(jnp.float32) / 128.0).reshape(
        rows, exps.shape[1], codes.shape[1] // exps.shape[1]
    )
    return (values * scale[:, :, None]).reshape(rows, codes.shape[1])


def body(acts, out_grad, projection, weight, m_codes, m_exps, v_codes, v_exps, next_acts):
    col_width = acts.shape[1]
    col_start = lax.axis_index("col") * col_width
    proj_cols = lax.dynamic_slice_in_dim(projection, col_start, col_width, 0)
    partial_value = jnp.dot(acts, proj_cols, preferred_element_type=jnp.float32)
    lowrank = over_copies(partial_value, "col").astype(jnp.bfloat16)
    tokens_all = acts.shape[0] * lax.axis_size(DP)
    grad = (
        sum_at_owner(
            lax.dot_general(
                lowrank, out_grad, (((0,), (0,)), ((), ())), preferred_element_type=jnp.float32
            ),
            DP,
            0,
        )
        / tokens_all
    )
    m_old = decode(m_codes, m_exps)
    v_old = decode(v_codes, v_exps)
    first = beta_one * m_old + (1.0 - beta_one) * grad
    second = beta_two * v_old + (1.0 - beta_two) * grad * grad
    update = first / correct_first / (jnp.sqrt(second / correct_second) + epsilon)
    direction = update.astype(jnp.bfloat16)
    full_next = lax.all_gather(next_acts, "col", axis=1, tiled=True)
    row_count = weight.shape[0]
    row_start = lax.axis_index(DP) * row_count
    old_full = gathered_by_axis(weight, DP, (0, 1, 2), 0)
    dir_full = collect(direction, DP, 0)
    delta_full = jnp.dot(projection, dir_full, preferred_element_type=jnp.float32)
    full_weight = (old_full.astype(jnp.float32) - learn_rate * delta_full).astype(jnp.bfloat16)
    new_weight = lax.dynamic_slice_in_dim(full_weight, row_start, row_count, 0)
    result = jnp.dot(full_next, full_weight, preferred_element_type=jnp.float32)
    return (result.astype(jnp.bfloat16), new_weight, update)


def solution(mesh):
    torus = Mesh(mesh.devices.reshape(mesh.shape["col"], 2, 4, 4), ("col", "dp_0", "dp_1", "dp_2"))
    return jax.shard_map(
        body,
        mesh=torus,
        in_specs=(
            P(DP, "col"),
            P(DP, "col"),
            P(),
            P(DP, "col"),
            P(DP, "col"),
            P(DP, "col"),
            P(DP, "col"),
            P(DP, "col"),
            P(DP, "col"),
        ),
        out_specs=(P(DP, "col"), P(DP, "col"), P(DP, "col")),
        check_vma=False,
    )
```

profile of v0, /device:TPU:2, one launch (start us, length us, event | category | flops | bytes accessed | tf_op | source)
XLA Modules:
  0.0 285.9 jit_solution(1275187251293601851)
XLA Ops:
  7.2 0.0 copy-start
  7.2 0.0 all-gather.5.cloned.1.call-start
  7.2 21.9 %all-gather = bf16[320,1024]{1,0:T(8,128)(2,1)} all-gather(bf16[160,1024]{1,0:T(8,128)(2,1)} %param.12), channel_id=2, replica_groups=mesh['col'=8,'dp_0'=2,'dp_1'=4,'dp_2'=4] {'dp_0'}, dimensions={0}, use_global_device_ids=true | all-gather | bytes 983040 | tf_op jit(solution)/shard_map/all_gather | solution.py:49
  29.1 0.0 all-gather.5.cloned.1.call-update
  29.2 0.0 all-gather.7.cloned.1.call-start
  29.2 39.9 %all-gather.5.cloned.1.call-done = bf16[8,160,1024]{2,1,0:T(8,128)(2,1)} async-done(((bf16[2,160,1024]{2,1,0:T(8,128)(2,1)}), bf16[8,160,1024]{2,1,0:T(8,128)(2,1)}) %all-gather.5.cloned.1.call-update) | async-done | bytes 2621456 | tf_op jit(solution)/shard_map/all_gather | solution.py:49
  69.1 0.0 all-gather.7.cloned.1.call-update
  69.1 0.0 copy-start.4
  69.1 0.0 copy-start.5
  69.2 0.0 copy-done
  69.2 0.0 copy-start.2
  69.2 0.0 copy-start.3
  69.2 1.4 convolution_bitcast_fusion.1
  70.6 0.2 copy.26
  70.8 2.0 broadcast_in_dim.7
  72.8 0.0 copy-start.1
  72.8 4.9 %all-to-all-start = ((f32[8,384,256]{2,1,0:T(8,128)}), f32[8,384,256]{2,1,0:T(8,128)}, u32[]{:S(2)}, u32[]{:S(2)}) async-start(f32[8,384,256]{2,1,0:T(8,128)} %broadcast_in_dim.7), calls=%async_computation | async-start | bytes 6291456 | tf_op jit(solution)/shard_map/all_to_all | solution.py:18
  77.7 0.0 all-gather.9.cloned.1.call-start
  77.8 0.7 all-gather.9.cloned.1.call-update
  78.5 70.9 %all-to-all-done = f32[8,384,256]{2,1,0:T(8,128)} async-done(((f32[8,384,256]{2,1,0:T(8,128)}), f32[8,384,256]{2,1,0:T(8,128)}, u32[]{:S(2)}, u32[]{:S(2)}) %all-to-all-start) | async-done | bytes 3145760 | tf_op jit(solution)/shard_map/all_to_all | solution.py:18
  149.4 2.9 reduce_sum.18
  152.2 0.0 copy-done.1
  152.2 2.4 convolution_bitcast_fusion
  154.6 11.0 %all-to-all-start.1 = ((f32[32,8,1024]{2,1,0:T(8,128)}), f32[32,8,1024]{2,1,0:T(8,128)}, u32[]{:S(2)}, u32[]{:S(2)}) async-start(f32[32,8,1024]{2,1,0:T(8,128)} %convolution_bitcast_fusion), calls=%async_computation.1 | async-start | bytes 2097152 | tf_op jit(solution)/shard_map/all_to_all | solution.py:36
  165.6 0.0 copy-done.4
  165.6 0.1 mul.78
  165.7 0.1 mul.79
  165.8 0.0 copy-done.5
  165.8 0.1 mul.70
  165.9 0.1 mul.71
  166.1 27.5 %all-to-all-done.1 = f32[32,8,1024]{2,1,0:T(8,128)} async-done(((f32[32,8,1024]{2,1,0:T(8,128)}), f32[32,8,1024]{2,1,0:T(8,128)}, u32[]{:S(2)}, u32[]{:S(2)}) %all-to-all-start.1) | async-done | bytes 1048608 | tf_op jit(solution)/shard_map/all_to_all | solution.py:36
  193.5 1.3 reduce_sum.19
  194.8 0.0 copy-done.2
  194.8 0.0 copy-done.3
  194.9 0.7 fusion.6
  195.5 0.9 broadcast_in_dim.8
  196.4 7.9 %all-to-all-start.2 = ((bf16[32,8,1024]{2,1,0:T(8,128)(2,1)}), bf16[32,8,1024]{2,1,0:T(8,128)(2,1)S(1)}, u32[]{:S(2)}, u32[]{:S(2)}) async-start(bf16[32,8,1024]{2,1,0:T(8,128)(2,1)} %broadcast_in_dim.8), calls=%async_computation.2 | async-start | bytes 1048576 | tf_op jit(solution)/shard_map/all_to_all | solution.py:18
  204.3 0.0 all-gather.7.cloned.1.call-done
  204.3 13.8 %convert_bitcast_fusion = f32[2,4,4,160,1024]{4,3,0,1,2:T(8,128)} fusion(bf16[4,4,2,160,1024]{4,3,2,1,0:T(8,128)(2,1)} %bitcast.26), kind=kLoop, calls=%fused_computation | loop fusion | flops 5242880 | bytes 31457280 | tf_op jit(solution)/shard_map/convert_element_type | solution.py:103
  218.1 16.5 %copy.25 = f32[2,4,4,160,1024]{4,3,2,1,0:T(8,128)} copy(f32[2,4,4,160,1024]{4,3,0,1,2:T(8,128)} %convert_bitcast_fusion) | data formatting | bytes 41943040 | tf_op jit(solution)/shard_map/convert_element_type | solution.py:103
  234.6 20.0 %copy.27 = f32[5120,1024]{0,1:T(8,128)} copy(f32[5120,1024]{1,0:T(8,128)} %bitcast.25) | data formatting | bytes 41943040 | tf_op jit(solution)/shard_map/convert_element_type | solution.py:103
  254.6 0.0 all-to-all-done.2
  254.6 11.8 %fusion = bf16[5120,1024]{0,1:T(8,128)(2,1)} fusion(f32[5120,1024]{0,1:T(8,128)} %copy.27, bf16[5120,256]{1,0:T(8,128)(2,1)S(1)} %copy-done, bf16[32,8,1024]{2,1,0:T(8,128)(2,1)S(1)} %all-to-all-done.2), kind=kOutput, calls=%fused_computation.2 | convolution fusion | flops 2700083200 | bytes 34603008 | tf_op jit(solution)/shard_map/dot_general | solution.py:102
  266.4 0.0 all-gather.9.cloned.1.call-done
  266.4 9.5 %fusion.1 = bf16[384,1024]{0,1:T(8,128)(2,1)S(1)} fusion(bf16[5120,1024]{0,1:T(8,128)(2,1)} %fusion, bf16[384,5120]{1,0:T(8,128)(2,1)} %all-gather.9.cloned.1.call-done), kind=kOutput, calls=%fused_computation.5 | convolution fusion | flops 4026925056 | bytes 15204352 | tf_op jit(solution)/shard_map/dot_general | solution.py:105
  275.9 1.2 copy.28
  277.1 1.4 constant_dynamic-slice_fusion
  278.4 0.9 copy.29
  (2 shorter events, 0.0 us)
Async XLA Ops:
  7.2 62.0 %copy-start = (bf16[5120,256]{1,0:T(8,128)(2,1)S(1)}, bf16[5120,256]{1,0:T(8,128)(2,1)}, u32[]{:S(2)}) copy-start(bf16[5120,256]{1,0:T(8,128)(2,1)} %param.11) | copy-start | bytes 7864324
  7.2 61.9 %all-gather.5.cloned.1.call-start = ((), (), s32[]{:S(2)}) async-start(), calls=%async_computation.3 | async-start | bytes 3276800 | tf_op jit(solution)/shard_map/all_gather | solution.py:49
  29.2 175.1 %all-gather.7.cloned.1.call-start = ((), (), s32[]{:S(2)}) async-start(), calls=%async_computation.4 | async-start | bytes 13107200 | tf_op jit(solution)/shard_map/all_gather | solution.py:49
  69.1 96.5 %copy-start.4 = (s32[8,32]{1,0:T(8,128)S(1)}, s32[8,32]{1,0:T(8,128)}, u32[]{:S(2)}) copy-start(s32[8,32]{1,0:T(8,128)} %param.16) | copy-start | bytes 3076
  69.1 96.7 %copy-start.5 = (s32[8,32]{1,0:T(8,128)S(1)}, s32[8,32]{1,0:T(8,128)}, u32[]{:S(2)}) copy-start(s32[8,32]{1,0:T(8,128)} %param.14) | copy-start | bytes 3076
  69.2 125.7 %copy-start.2 = (s32[8,1024]{1,0:T(8,128)S(1)}, s32[8,1024]{1,0:T(8,128)}, u32[]{:S(2)}) copy-start(s32[8,1024]{1,0:T(8,128)} %param.15) | copy-start | bytes 98308
  69.2 125.7 %copy-start.3 = (s32[8,1024]{1,0:T(8,128)S(1)}, s32[8,1024]{1,0:T(8,128)}, u32[]{:S(2)}) copy-start(s32[8,1024]{1,0:T(8,128)} %param.13) | copy-start | bytes 98308
  72.8 79.4 %copy-start.1 = (bf16[384,1024]{1,0:T(8,128)(2,1)S(1)}, bf16[384,1024]{1,0:T(8,128)(2,1)}, u32[]{:S(2)}) copy-start(bf16[384,1024]{1,0:T(8,128)(2,1)} %param.10) | copy-start | bytes 2359300
  72.8 76.6 %all-to-all-start = ((f32[8,384,256]{2,1,0:T(8,128)}), f32[8,384,256]{2,1,0:T(8,128)}, u32[]{:S(2)}, u32[]{:S(2)}) async-start(f32[8,384,256]{2,1,0:T(8,128)} %broadcast_in_dim.7), calls=%async_computation | async-start | bytes 6291456 | tf_op jit(solution)/shard_map/all_to_all | solution.py:18
  77.7 188.7 %all-gather.9.cloned.1.call-start = ((), (), s32[]{:S(2)}) async-start(), calls=%async_computation.5 | async-start | bytes 4423680 | tf_op jit(solution)/shard_map/all_gather | solution.py:97
  154.6 39.0 %all-to-all-start.1 = ((f32[32,8,1024]{2,1,0:T(8,128)}), f32[32,8,1024]{2,1,0:T(8,128)}, u32[]{:S(2)}, u32[]{:S(2)}) async-start(f32[32,8,1024]{2,1,0:T(8,128)} %convolution_bitcast_fusion), calls=%async_computation.1 | async-start | bytes 2097152 | tf_op jit(solution)/shard_map/all_to_all | solution.py:36
  196.4 58.2 %all-to-all-start.2 = ((bf16[32,8,1024]{2,1,0:T(8,128)(2,1)}), bf16[32,8,1024]{2,1,0:T(8,128)(2,1)S(1)}, u32[]{:S(2)}, u32[]{:S(2)}) async-start(bf16[32,8,1024]{2,1,0:T(8,128)(2,1)} %broadcast_in_dim.8), calls=%async_computation.2 | async-start | bytes 1048576 | tf_op jit(solution)/shard_map/all_to_all | solution.py:18
Sparse Core Ops, SparseCore 0:
  29.3 39.7 all-gather.4
  70.9 111.1 all-gather.6
  184.0 67.3 all-gather.8
where the time goes:
time: 287 us; the launch traced here: 286 us
  waiting for transfers between devices  139 us (48%)
  local copies, waits for them, and re-layouts  43.4 us (15%)
  matrix products  25.1 us (9%)
  starting transfers between devices  23.9 us (8%)
  blocking collectives  21.9 us (8%)
  other arithmetic  18.6 us (6%)
  between operations  13.9 us (5%)
    all_to_all x2, waiting for transfers between devices, sent_to_all(): lax.all_to_all(jnp.broadcast_to(shard[None], (size, *shard.shape)), axis,...  70.9 us
    all_gather x2, waiting for transfers between devices, gather_in_order(): pieces = lax.all_gather(pieces, axes[k], axis=0, tiled=True)  39.9 us
    convert_element_type x2, local copies, waits for them, and re-layouts, body(): old_full.astype(jnp.float32) - learn_rate * delta_full  36.5 us
    all_to_all x1, waiting for transfers between devices, sum_at_owner(): lax.all_to_all(pieces, axis, split_axis=0, concat_axis=0, tiled=True)  27.5 us
    all_gather x1, blocking collectives, gather_in_order(): pieces = lax.all_gather(pieces, axes[k], axis=0, tiled=True)  21.9 us
    convert_element_type x1, other arithmetic, body(): old_full.astype(jnp.float32) - learn_rate * delta_full  13.8 us
    all_to_all x2, starting transfers between devices, sent_to_all(): lax.all_to_all(jnp.broadcast_to(shard[None], (size, *shard.shape)), axis,...  12.8 us
    dot_general x1, matrix products, body(): jnp.dot(projection, dir_full, preferred_element_type=jnp.float32)  11.8 us
  transfers between devices with their start and end apart: 6, of which 3 were waited for; matrix products, arithmetic and copies ran while one was open for 26% of the time, Pallas kernels for 0%

commit v1 on v0

--- a/solution.py
+++ b/solution.py
@@ -3,6 +3,7 @@
 from jax import lax
 from jax.sharding import Mesh
 from jax.sharding import PartitionSpec as P
+from jax.lax import all_to_all, axis_size
 
 DP = ("dp_0", "dp_1", "dp_2")
 learn_rate = 0.02
@@ -46,7 +47,10 @@
 def gather_in_order(shard, axes, sequence):
     pieces = shard[None]
     for k in sequence:
-        pieces = lax.all_gather(pieces, axes[k], axis=0, tiled=True)
+        row_data = axes[k]
+        pieces = jnp.concatenate(
+            all_to_all(jnp.stack([pieces] * axis_size(row_data)), row_data, 0, 0), axis=0
+        )
     block = [lax.axis_size(axes[k]) for k in reversed(sequence)]
     pieces = pieces.reshape(*block, *shard.shape)
     turned = sorted(range(len(sequence)), key=lambda place: sequence[len(sequence) - 1 - place])

time: 287 us -> 403 us (1.40)
  blocking collectives: 21.9 us -> 108 us
  waiting for transfers between devices: 139 us -> 152 us
  local copies, waits for them, and re-layouts: 43.4 us -> 53.3 us
  starting transfers between devices: 23.9 us -> 29 us
    all_to_all x1 -> x3, waiting for transfers between devices: 27.5 us -> 151 us  [gather_in_order(): all_to_all(jnp.stack([pieces] * axis_size(row_data)), row_data, 0, 0)]
    all_to_all x0 -> x2, blocking collectives: none -> 108 us  [the longest x1 74.9 us: sent_to_all(): lax.all_to_all(jnp.broadcast_to(shard[None], (size, *shard.shape)), axis,...]
    all_to_all x2 -> x1, waiting for transfers between devices: 70.9 us -> 0.01 us  [sent_to_all(): lax.all_to_all(jnp.broadcast_to(shard[None], (size, *shard.shape)), axis,...]
    all_gather x2 -> x0, waiting for transfers between devices: 39.9 us -> none  [gather_in_order(): pieces = lax.all_gather(pieces, axes[k], axis=0, tiled=True)]
    all_gather x1 -> x0, blocking collectives: 21.9 us -> none  [gather_in_order(): pieces = lax.all_gather(pieces, axes[k], axis=0, tiled=True)]
    all_to_all x1 -> x3, starting transfers between devices: 11 us -> 20.5 us  [gather_in_order(): all_to_all(jnp.stack([pieces] * axis_size(row_data)), row_data, 0, 0)]
    another operation x0 -> x2, local copies, waits for them, and re-layouts: none -> 9.07 us  [gather_in_order(): jnp.stack([pieces] * axis_size(row_data))]
    all_to_all x2 -> x1, starting transfers between devices: 12.8 us -> 8.48 us  [sent_to_all(): lax.all_to_all(jnp.broadcast_to(shard[None], (size, *shard.shape)), axis,...]
  transfers between devices with their start and end apart: 6 -> 5, of which waited for: 3 -> 3; matrix products, arithmetic and copies ran while one was open for 26% -> 18% of each run, Pallas kernels for 0% -> 0%
where the time goes in v1:
time: 403 us; the launch traced here: 402 us
  waiting for transfers between devices  152 us (38%)
  blocking collectives  108 us (27%)
  local copies, waits for them, and re-layouts  53.3 us (13%)
  starting transfers between devices  29 us (7%)
  matrix products  26 us (6%)
  other arithmetic  19.9 us (5%)
  between operations  14.2 us (4%)
    all_to_all x3, waiting for transfers between devices, gather_in_order(): all_to_all(jnp.stack([pieces] * axis_size(row_data)), row_data, 0, 0)  151 us
    all_to_all x1, blocking collectives, sent_to_all(): lax.all_to_all(jnp.broadcast_to(shard[None], (size, *shard.shape)), axis,...  74.9 us
    convert_element_type x2, local copies, waits for them, and re-layouts, body(): old_full.astype(jnp.float32) - learn_rate * delta_full  36.3 us
    all_to_all x1, blocking collectives, sum_at_owner(): lax.all_to_all(pieces, axis, split_axis=0, concat_axis=0, tiled=True)  32.6 us
    all_to_all x3, starting transfers between devices, gather_in_order(): all_to_all(jnp.stack([pieces] * axis_size(row_data)), row_data, 0, 0)  20.5 us
    convert_element_type x1, other arithmetic, body(): old_full.astype(jnp.float32) - learn_rate * delta_full  13.7 us
    dot_general x1, matrix products, body(): jnp.dot(projection, dir_full, preferred_element_type=jnp.float32)  11.8 us
    dot_general x1, matrix products, body(): result = jnp.dot(full_next, full_weight, preferred_element_type=jnp.float32)  9.48 us
  transfers between devices with their start and end apart: 5, of which 3 were waited for; matrix products, arithmetic and copies ran while one was open for 18% of the time, Pallas kernels for 0%

profile of v1, /device:TPU:2, one launch (start us, length us, event | category | flops | bytes accessed | tf_op | source)
XLA Modules:
  0.0 401.9 jit_solution(10962381859534769749)
XLA Ops:
  7.2 0.0 copy-start
  7.2 2.1 pad_maximum_fusion
  9.3 8.5 %all-to-all-start = ((bf16[2,1,160,1024]{3,2,1,0:T(8,128)(2,1)}), bf16[2,1,160,1024]{3,2,1,0:T(8,128)(2,1)S(1)}, u32[]{:S(2)}, u32[]{:S(2)}) async-start(bf16[2,1,160,1024]{3,2,1,0:T(8,128)(2,1)} %pad_maximum_fusion), calls=%async_computation | async-start | bytes 1310720 | tf_op jit(solution)/shard_map/all_to_all | solution.py:52
  17.8 0.0 copy-done
  17.8 2.2 convolution_bitcast_fusion.1
  19.9 1.9 copy.21
  21.8 15.4 %all-to-all-done = bf16[2,1,160,1024]{3,2,1,0:T(8,128)(2,1)S(1)} async-done(((bf16[2,1,160,1024]{3,2,1,0:T(8,128)(2,1)}), bf16[2,1,160,1024]{3,2,1,0:T(8,128)(2,1)S(1)}, u32[]{:S(2)}, u32[]{:S(2)}) %all-to-all-start) | async-done | bytes 655392 | tf_op jit(solution)/shard_map/all_to_all | solution.py:52
  37.2 1.3 broadcast_in_dim.4
  38.4 74.9 %all_to_all.30 = f32[8,384,256]{2,1,0:T(8,128)} all-to-all(f32[8,384,256]{2,1,0:T(8,128)S(1)} %broadcast_in_dim.4), channel_id=1, replica_groups=mesh['col'=8,'dp_0'=2,'dp_1'=4,'dp_2'=4] {'col'}, dimensions={0} | all-to-all | bytes 6291456 | tf_op jit(solution)/shard_map/all_to_all | solution.py:19
  113.4 1.9 stack.10
  115.2 4.5 %all-to-all-start.1 = ((bf16[4,2,160,1024]{3,2,1,0:T(8,128)(2,1)}), bf16[4,2,160,1024]{3,2,1,0:T(8,128)(2,1)}, u32[]{:S(2)}, u32[]{:S(2)}) async-start(bf16[4,2,160,1024]{3,2,1,0:T(8,128)(2,1)} %stack.10), calls=%async_computation.1 | async-start | bytes 5242880 | tf_op jit(solution)/shard_map/all_to_all | solution.py:52
  119.8 2.1 reduce_sum.18
  121.9 2.6 convolution_bitcast_fusion
  124.5 27.2 %all-to-all-done.1 = bf16[4,2,160,1024]{3,2,1,0:T(8,128)(2,1)} async-done(((bf16[4,2,160,1024]{3,2,1,0:T(8,128)(2,1)}), bf16[4,2,160,1024]{3,2,1,0:T(8,128)(2,1)}, u32[]{:S(2)}, u32[]{:S(2)}) %all-to-all-start.1) | async-done | bytes 2621472 | tf_op jit(solution)/shard_map/all_to_all | solution.py:52
  151.7 32.6 %all_to_all.31 = f32[32,8,1024]{2,1,0:T(8,128)} all-to-all(f32[32,8,1024]{2,1,0:T(8,128)} %convolution_bitcast_fusion), channel_id=1, replica_groups=mesh['col'=8,'dp_0'=2,'dp_1'=4,'dp_2'=4] {'dp_0','dp_1','dp_2'}, dimensions={0} | all-to-all | bytes 2097152 | tf_op jit(solution)/shard_map/all_to_all | solution.py:37
  184.3 7.2 %stack.11 = bf16[4,8,160,1024]{3,2,1,0:T(8,128)(2,1)} broadcast(bf16[8,160,1024]{2,1,0:T(8,128)(2,1)} %bitcast.2), dimensions={1,2,3} | broadcast | bytes 13107200 | tf_op jit(solution)/shard_map/stack | solution.py:52
  191.5 0.0 copy-start.3
  191.5 0.0 copy-start.4
  191.6 0.0 copy-start.1
  191.6 0.0 copy-start.2
  191.6 7.5 %all-to-all-start.2 = ((bf16[4,8,160,1024]{3,2,1,0:T(8,128)(2,1)}), bf16[4,8,160,1024]{3,2,1,0:T(8,128)(2,1)}, u32[]{:S(2)}, u32[]{:S(2)}) async-start(bf16[4,8,160,1024]{3,2,1,0:T(8,128)(2,1)} %stack.11), calls=%async_computation.2 | async-start | bytes 20971520 | tf_op jit(solution)/shard_map/all_to_all | solution.py:52
  199.1 0.0 all-gather.2.cloned.1.call-start
  199.1 0.7 all-gather.2.cloned.1.call-update
  199.8 0.0 copy-done.3
  199.8 0.1 mul.78
  199.9 0.1 mul.79
  200.0 0.0 copy-done.4
  200.0 0.1 mul.70
  200.1 0.1 mul.71
  200.2 1.3 reduce_sum.19
  201.5 0.0 copy-done.1
  201.5 0.0 copy-done.2
  201.6 0.7 fusion.6
  202.2 108.6 %all-to-all-done.2 = bf16[4,8,160,1024]{3,2,1,0:T(8,128)(2,1)} async-done(((bf16[4,8,160,1024]{3,2,1,0:T(8,128)(2,1)}), bf16[4,8,160,1024]{3,2,1,0:T(8,128)(2,1)}, u32[]{:S(2)}, u32[]{:S(2)}) %all-to-all-start.2) | async-done | bytes 10485792 | tf_op jit(solution)/shard_map/all_to_all | solution.py:52
  310.9 0.9 broadcast_in_dim.5
  311.7 8.5 %all-to-all-start.5 = ((bf16[32,8,1024]{2,1,0:T(8,128)(2,1)}), bf16[32,8,1024]{2,1,0:T(8,128)(2,1)S(1)}, u32[]{:S(2)}, u32[]{:S(2)}) async-start(bf16[32,8,1024]{2,1,0:T(8,128)(2,1)} %broadcast_in_dim.5), calls=%async_computation.5 | async-start | bytes 1048576 | tf_op jit(solution)/shard_map/all_to_all | solution.py:19
  320.2 13.7 %convert_bitcast_fusion = f32[2,4,4,160,1024]{4,3,0,1,2:T(8,128)} fusion(bf16[4,4,2,160,1024]{4,3,2,1,0:T(8,128)(2,1)} %bitcast.11), kind=kLoop, calls=%fused_computation | loop fusion | flops 5242880 | bytes 31457280 | tf_op jit(solution)/shard_map/convert_element_type | solution.py:107
  333.9 16.4 %copy.20 = f32[2,4,4,160,1024]{4,3,2,1,0:T(8,128)} copy(f32[2,4,4,160,1024]{4,3,0,1,2:T(8,128)} %convert_bitcast_fusion) | data formatting | bytes 41943040 | tf_op jit(solution)/shard_map/convert_element_type | solution.py:107
  350.3 19.9 %copy.22 = f32[5120,1024]{0,1:T(8,128)} copy(f32[5120,1024]{1,0:T(8,128)} %bitcast.27) | data formatting | bytes 41943040 | tf_op jit(solution)/shard_map/convert_element_type | solution.py:107
  370.3 0.0 all-to-all-done.5
  370.3 11.8 %fusion = bf16[5120,1024]{0,1:T(8,128)(2,1)} fusion(f32[5120,1024]{0,1:T(8,128)} %copy.22, bf16[5120,256]{1,0:T(8,128)(2,1)S(1)} %copy-done, bf16[32,8,1024]{2,1,0:T(8,128)(2,1)S(1)} %all-to-all-done.5), kind=kOutput, calls=%fused_computation.2 | convolution fusion | flops 2700083200 | bytes 34603008 | tf_op jit(solution)/shard_map/dot_general | solution.py:106
  382.1 0.0 all-gather.2.cloned.1.call-done
  382.1 9.5 %fusion.1 = bf16[384,1024]{0,1:T(8,128)(2,1)S(1)} fusion(bf16[5120,1024]{0,1:T(8,128)(2,1)} %fusion, bf16[384,5120]{1,0:T(8,128)(2,1)} %all-gather.2.cloned.1.call-done), kind=kOutput, calls=%fused_computation.5 | convolution fusion | flops 4026925056 | bytes 15204352 | tf_op jit(solution)/shard_map/dot_general | solution.py:109
  391.6 1.2 copy.23
  392.7 1.4 constant_dynamic-slice_fusion
  394.1 0.9 copy.24
  (2 shorter events, 0.0 us)
Async XLA Ops:
  7.2 10.6 %copy-start = (bf16[5120,256]{1,0:T(8,128)(2,1)S(1)}, bf16[5120,256]{1,0:T(8,128)(2,1)}, u32[]{:S(2)}) copy-start(bf16[5120,256]{1,0:T(8,128)(2,1)} %param.11) | copy-start | bytes 7864324
  9.3 27.9 %all-to-all-start = ((bf16[2,1,160,1024]{3,2,1,0:T(8,128)(2,1)}), bf16[2,1,160,1024]{3,2,1,0:T(8,128)(2,1)S(1)}, u32[]{:S(2)}, u32[]{:S(2)}) async-start(bf16[2,1,160,1024]{3,2,1,0:T(8,128)(2,1)} %pad_maximum_fusion), calls=%async_computation | async-start | bytes 1310720 | tf_op jit(solution)/shard_map/all_to_all | solution.py:52
  115.2 36.5 %all-to-all-start.1 = ((bf16[4,2,160,1024]{3,2,1,0:T(8,128)(2,1)}), bf16[4,2,160,1024]{3,2,1,0:T(8,128)(2,1)}, u32[]{:S(2)}, u32[]{:S(2)}) async-start(bf16[4,2,160,1024]{3,2,1,0:T(8,128)(2,1)} %stack.10), calls=%async_computation.1 | async-start | bytes 5242880 | tf_op jit(solution)/shard_map/all_to_all | solution.py:52
  191.5 8.2 %copy-start.3 = (s32[8,32]{1,0:T(8,128)S(1)}, s32[8,32]{1,0:T(8,128)}, u32[]{:S(2)}) copy-start(s32[8,32]{1,0:T(8,128)} %param.16) | copy-start | bytes 3076
  191.5 8.5 %copy-start.4 = (s32[8,32]{1,0:T(8,128)S(1)}, s32[8,32]{1,0:T(8,128)}, u32[]{:S(2)}) copy-start(s32[8,32]{1,0:T(8,128)} %param.14) | copy-start | bytes 3076
  191.6 10.0 %copy-start.1 = (s32[8,1024]{1,0:T(8,128)S(1)}, s32[8,1024]{1,0:T(8,128)}, u32[]{:S(2)}) copy-start(s32[8,1024]{1,0:T(8,128)} %param.15) | copy-start | bytes 98308
  191.6 10.0 %copy-start.2 = (s32[8,1024]{1,0:T(8,128)S(1)}, s32[8,1024]{1,0:T(8,128)}, u32[]{:S(2)}) copy-start(s32[8,1024]{1,0:T(8,128)} %param.13) | copy-start | bytes 98308
  191.6 119.3 %all-to-all-start.2 = ((bf16[4,8,160,1024]{3,2,1,0:T(8,128)(2,1)}), bf16[4,8,160,1024]{3,2,1,0:T(8,128)(2,1)}, u32[]{:S(2)}, u32[]{:S(2)}) async-start(bf16[4,8,160,1024]{3,2,1,0:T(8,128)(2,1)} %stack.11), calls=%async_computation.2 | async-start | bytes 20971520 | tf_op jit(solution)/shard_map/all_to_all | solution.py:52
  199.1 183.0 %all-gather.2.cloned.1.call-start = ((), (), s32[]{:S(2)}) async-start(), calls=%async_computation.6 | async-start | bytes 4423680 | tf_op jit(solution)/shard_map/all_gather | solution.py:101
  311.7 58.5 %all-to-all-start.5 = ((bf16[32,8,1024]{2,1,0:T(8,128)(2,1)}), bf16[32,8,1024]{2,1,0:T(8,128)(2,1)S(1)}, u32[]{:S(2)}, u32[]{:S(2)}) async-start(bf16[32,8,1024]{2,1,0:T(8,128)(2,1)} %broadcast_in_dim.5), calls=%async_computation.5 | async-start | bytes 1048576 | tf_op jit(solution)/shard_map/all_to_all | solution.py:19
Sparse Core Ops, SparseCore 0:
  201.6 50.0 all-gather.1
